TPU v7x, 32 devices: a whole 2x2x4 slice. The times are simulated.
32 devices in a mesh: groups: 2 (over y), row: 4 (over x, core), col: 4 (over z).
Axes of the slice: x: 2, y: 2, z: 4, core: 2. Of those that a mesh axis runs over, the one named last changes fastest.
Arguments:
- inputs: bfloat16 [1536, 4096], P(('groups', 'col'), 'row'), parts along dimension 0, may hold values from -6 to 6
- cotangent: bfloat16 [1536, 4096], P(('groups', 'col'), 'row'), parts along dimension 0, may hold values from -6 to 6
- preactivation: bfloat16 [1536, 8192], P(('groups', 'row'), 'col'), parts along dimension 0, may hold values from -8 to 8
- up_weight: bfloat16 [4096, 8192], P('row', 'col'), may hold values from -0.09375 to 0.09375
- down_weight: bfloat16 [8192, 4096], P('col', 'row'), may hold values from -0.0625 to 0.0625
Outputs:
- grad_input: bfloat16 [1536, 4096], P(('groups', 'col'), 'row'), parts along dimension 0
- grad_up: float32 [8192, 8192], P(('groups', 'row'), 'col'), parts along dimension 0
- grad_down: float32 [16384, 4096], P(('groups', 'col'), 'row'), parts along dimension 0
There are 2 independent parts, one for each index of `groups`. A program takes and returns all parts, laid end to end along the dimension named above; an argument that names none is the same for every part. Nothing has to cross between parts.
All inputs are finite; a program needn't handle non-finite values.
Results may differ from a plain program's by a relative error of at most 0.0049.
Values may be sent and summed in bfloat16 or wider, within the bound.
A program may use at most 128 MiB of HBM per device.

v0:
```python
import math
import jax
import jax.numpy as jnp
from jax import lax
from jax.sharding import PartitionSpec as P


def gelu_pair(values):
    v = values.astype(jnp.float32)
    tanh_arg = 0.7978845608 * (v + 0.044715 * v * v * v)
    tanh_val = jnp.tanh(tanh_arg)
    gelu_value = 0.5 * v * (1.0 + tanh_val)
    gelu_slope = 0.5 * (1.0 + tanh_val) + 0.5 * v * (1.0 - tanh_val * tanh_val) * 0.7978845608 * (
        1.0 + 3.0 * 0.044715 * v * v
    )
    return (gelu_value, gelu_slope)


def per_device(inputs, cotangent, preactivation, up_weight, down_weight):
    inputs_all, cotangent_all = (
        lax.all_gather(inputs, "col", axis=0, tiled=True),
        lax.all_gather(cotangent, "col", axis=0, tiled=True),
    )
    total_tokens = inputs_all.shape[0]
    token_scale = 1.0 / math.sqrt(total_tokens)
    last_dims = (((1,), (1,)), ((), ()))
    first_dims = (((0,), (0,)), ((), ()))
    piece = cotangent_all
    hidden_grad = lax.psum_scatter(
        lax.dot_general(piece, down_weight, last_dims, preferred_element_type=jnp.float32),
        "row",
        scatter_dimension=0,
        tiled=True,
    )
    gelu_value, gelu_slope = gelu_pair(preactivation)
    activation = gelu_value.astype(jnp.bfloat16)
    pre_grad = (hidden_grad * gelu_slope).astype(jnp.bfloat16)
    activation_all, pre_grad_all = (
        lax.all_gather(activation, "row", axis=0, tiled=True),
        lax.all_gather(pre_grad, "row", axis=0, tiled=True),
    )
    piece = pre_grad_all
    grad_input = lax.psum_scatter(
        lax.dot_general(piece, up_weight, last_dims, preferred_element_type=jnp.float32),
        "col",
        scatter_dimension=0,
        tiled=True,
    ).astype(jnp.bfloat16)
    grad_up = (
        lax.dot_general(inputs_all, pre_grad_all, first_dims, preferred_element_type=jnp.float32)
        * token_scale
    )
    grad_down = (
        lax.dot_general(
            activation_all, cotangent_all, first_dims, preferred_element_type=jnp.float32
        )
        * token_scale
    )
    return (grad_input, grad_up, grad_down)


def solution(mesh):
    placed = (
        P(("groups", "col"), "row"),
        P(("groups", "col"), "row"),
        P(("groups", "row"), "col"),
        P("row", "col"),
        P("col", "row"),
    )
    return jax.shard_map(
        per_device,
        mesh=mesh,
        in_specs=placed,
        out_specs=(
            P(("groups", "col"), "row"),
            P(("groups", "row"), "col"),
            P(("groups", "col"), "row"),
        ),
        check_vma=False,
    )
```

profile of v0, /device:TPU:0, one launch (start us, length us, event | category | flops | bytes accessed | tf_op | source)
XLA Modules:
  0.0 287.1 jit_solution(9059382792913873849)
XLA Ops:
  7.2 0.0 all-gather.5.cloned.1.call-start
  7.2 0.7 all-gather.5.cloned.1.call-update
  7.9 0.0 reduce-scatter.3.cloned.1.call-start
  7.9 41.4 %all-gather.5.cloned.1.call-done = bf16[768,1024]{1,0:T(8,128)(2,1)} async-done(((bf16[192,1024]{1,0:T(8,128)(2,1)}), bf16[768,1024]{1,0:T(8,128)(2,1)}) %all-gather.5.cloned.1.call-update) | async-done | bytes 1572880 | tf_op jit(solution)/shard_map/all_gather | solution.py:22
  49.3 8.8 %fusion.11 = f32[768,2048]{1,0:T(8,128)} fusion(bf16[768,1024]{1,0:T(8,128)(2,1)} %all-gather.5.cloned.1.call-done, bf16[2048,1024]{1,0:T(8,128)(2,1)} %param.9), kind=kOutput, calls=%fused_computation.20 | convolution fusion | flops 3221225472 | bytes 12058624 | tf_op jit(solution)/shard_map/dot_general | solution.py:30
  58.1 0.0 copy-start
  58.1 0.0 reduce-scatter.3.cloned.1.call-update
  58.2 0.0 all-gather.7.cloned.1.call-start
  58.2 57.8 %reduce-scatter.3.cloned.1.call-done = f32[192,2048]{1,0:T(8,128)} async-done(((f32[768,2048]{1,0:T(8,128)}), f32[192,2048]{1,0:T(8,128)}) %reduce-scatter.3.cloned.1.call-update) | async-done | bytes 1572880 | tf_op jit(solution)/shard_map/reduce_scatter | solution.py:29
  116.0 0.0 copy-done
  116.0 3.7 %fusion.7 = (bf16[192,2048]{1,0:T(8,128)(2,1)}, bf16[192,2048]{1,0:T(8,128)(2,1)}) fusion(bf16[192,2048]{1,0:T(8,128)(2,1)S(1)} %copy-done, f32[192,2048]{1,0:T(8,128)} %reduce-scatter.3.cloned.1.call-done), kind=kLoop, calls=%fused_computation.16 | loop fusion | flops 8650752 | bytes 3932160 | tf_op jit(solution)/shard_map/convert_element_type | solution.py:36
  119.7 0.0 all-gather.7.cloned.1.call-update
  119.7 0.0 all-gather.9.cloned.1.call-start
  119.8 0.5 all-gather.9.cloned.1.call-update
  120.3 0.0 all-gather.11.cloned.1.call-start
  120.4 0.5 all-gather.11.cloned.1.call-update
  120.9 0.0 reduce-scatter.5.cloned.1.call-start
  121.0 27.4 %all-gather.7.cloned.1.call-done = bf16[768,2048]{1,0:T(8,128)(2,1)} async-done(((bf16[192,2048]{1,0:T(8,128)(2,1)}), bf16[768,2048]{1,0:T(8,128)(2,1)}) %all-gather.7.cloned.1.call-update) | async-done | bytes 3145744 | tf_op jit(solution)/shard_map/all_gather | solution.py:40
  148.4 8.3 %fusion.12 = f32[768,1024]{1,0:T(8,128)} fusion(bf16[768,2048]{1,0:T(8,128)(2,1)} %all-gather.7.cloned.1.call-done, bf16[1024,2048]{1,0:T(8,128)(2,1)} %param.8), kind=kOutput, calls=%fused_computation.21 | convolution fusion | flops 3221225472 | bytes 10485760 | tf_op jit(solution)/shard_map/dot_general | solution.py:44
  156.7 0.0 copy-start.1
  156.7 0.0 reduce-scatter.5.cloned.1.call-update
  156.7 30.2 %all-gather.9.cloned.1.call-done = bf16[768,1024]{1,0:T(8,128)(2,1)} async-done(((bf16[192,1024]{1,0:T(8,128)(2,1)}), bf16[768,1024]{1,0:T(8,128)(2,1)}) %all-gather.9.cloned.1.call-update) | async-done | bytes 1572880 | tf_op jit(solution)/shard_map/all_gather | solution.py:21
  186.9 0.0 copy-done.1
  186.9 7.1 %multiply_bitcast_fusion = f32[1024,2048]{0,1:T(8,128)} fusion(bf16[768,2048]{1,0:T(8,128)(2,1)S(1)} %copy-done.1, bf16[768,1024]{1,0:T(8,128)(2,1)} %all-gather.9.cloned.1.call-done), kind=kOutput, calls=%fused_computation | convolution fusion | flops 3223322624 | bytes 13107200 | tf_op jit(solution)/shard_map/dot_general | solution.py:50
  194.0 0.0 copy-start.2
  194.0 9.4 %copy.8 = f32[1024,2048]{1,0:T(8,128)} copy(f32[1024,2048]{0,1:T(8,128)} %multiply_bitcast_fusion) | data formatting | bytes 16777216
  203.4 12.3 %all-gather.11.cloned.1.call-done = bf16[768,2048]{1,0:T(8,128)(2,1)} async-done(((bf16[192,2048]{1,0:T(8,128)(2,1)}), bf16[768,2048]{1,0:T(8,128)(2,1)}) %all-gather.11.cloned.1.call-update) | async-done | bytes 3145744 | tf_op jit(solution)/shard_map/all_gather | solution.py:39
  215.7 0.0 copy-done.2
  215.7 7.6 %convolution_multiply_fusion = f32[2048,1024]{1,0:T(8,128)} fusion(bf16[768,2048]{1,0:T(8,128)(2,1)} %all-gather.11.cloned.1.call-done, bf16[768,1024]{1,0:T(8,128)(2,1)S(1)} %copy-done.2), kind=kOutput, calls=%fused_computation.1 | convolution fusion | flops 3223322624 | bytes 13107200 | tf_op jit(solution)/shard_map/dot_general | solution.py:54
  223.3 55.0 %reduce-scatter.5.cloned.1.call-done = f32[192,1024]{1,0:T(8,128)} async-done(((f32[768,1024]{1,0:T(8,128)}), f32[192,1024]{1,0:T(8,128)}) %reduce-scatter.5.cloned.1.call-update) | async-done | bytes 786448 | tf_op jit(solution)/shard_map/reduce_scatter | solution.py:43
  278.3 1.9 convert_element_type.14
Async XLA Ops:
  7.2 42.2 %all-gather.5.cloned.1.call-start = ((), (), s32[]{:S(2)}) async-start(), calls=%async_computation.2 | async-start | bytes 1966080 | tf_op jit(solution)/shard_map/all_gather | solution.py:22
  7.9 108.1 %reduce-scatter.3.cloned.1.call-start = ((), (), s32[]{:S(2)}) async-start(), calls=%async_computation.3 | async-start | bytes 7864320 | tf_op jit(solution)/shard_map/reduce_scatter | solution.py:29
  58.1 57.9 %copy-start = (bf16[192,2048]{1,0:T(8,128)(2,1)S(1)}, bf16[192,2048]{1,0:T(8,128)(2,1)}, u32[]{:S(2)}) copy-start(bf16[192,2048]{1,0:T(8,128)(2,1)} %param.7) | copy-start | bytes 2359300
  58.2 90.2 %all-gather.7.cloned.1.call-start = ((), (), s32[]{:S(2)}) async-start(), calls=%async_computation.4 | async-start | bytes 3932160 | tf_op jit(solution)/shard_map/all_gather | solution.py:40
  119.7 67.1 %all-gather.9.cloned.1.call-start = ((), (), s32[]{:S(2)}) async-start(), calls=%async_computation.6 | async-start | bytes 1966080 | tf_op jit(solution)/shard_map/all_gather | solution.py:21
  120.3 95.4 %all-gather.11.cloned.1.call-start = ((), (), s32[]{:S(2)}) async-start(), calls=%async_computation.7 | async-start | bytes 3932160 | tf_op jit(solution)/shard_map/all_gather | solution.py:39
  120.9 157.4 %reduce-scatter.5.cloned.1.call-start = ((), (), s32[]{:S(2)}) async-start(), calls=%async_computation.5 | async-start | bytes 3932160 | tf_op jit(solution)/shard_map/reduce_scatter | solution.py:43
  156.7 30.2 %copy-start.1 = (bf16[768,2048]{1,0:T(8,128)(2,1)S(1)}, bf16[768,2048]{1,0:T(8,128)(2,1)}, u32[]{:S(2)}) copy-start(bf16[768,2048]{1,0:T(8,128)(2,1)} %all-gather.7.cloned.1.call-done) | copy-start | bytes 9437188
  194.0 21.7 %copy-start.2 = (bf16[768,1024]{1,0:T(8,128)(2,1)S(1)}, bf16[768,1024]{1,0:T(8,128)(2,1)}, u32[]{:S(2)}) copy-start(bf16[768,1024]{1,0:T(8,128)(2,1)} %all-gather.5.cloned.1.call-done) | copy-start | bytes 4718596
Sparse Core Ops, SparseCore 0:
  9.5 39.7 all-gather.4
  58.3 57.7 reduce-scatter.2
  119.9 28.4 all-gather.6
  149.8 37.0 all-gather.8
  188.3 27.3 all-gather.10
  217.9 60.3 reduce-scatter.4
where the time goes:
time: 287 us
  waiting for transfers between devices  226 us (79%)
  matrix products  31.8 us (11%)
  between operations  14.1 us (5%)
  local copies, waits for them, and re-layouts  9.45 us (3%)
  other arithmetic  5.61 us (2%)
    reduce_scatter x1, waiting for transfers between devices, per_device(): lax.psum_scatter(lax.dot_general(piece, down_weight, last_dims, preferred...  57.8 us
    reduce_scatter x1, waiting for transfers between devices, per_device(): lax.psum_scatter(lax.dot_general(piece, up_weight, last_dims, preferred_e...  55 us
    all_gather x1, waiting for transfers between devices, per_device(): lax.all_gather(cotangent, 'col', axis=0, tiled=True)  41.4 us
    all_gather x1, waiting for transfers between devices, per_device(): lax.all_gather(inputs, 'col', axis=0, tiled=True)  30.2 us
    all_gather x1, waiting for transfers between devices, per_device(): lax.all_gather(pre_grad, 'row', axis=0, tiled=True)  27.4 us
    all_gather x1, waiting for transfers between devices, per_device(): lax.all_gather(activation, 'row', axis=0, tiled=True)  12.3 us
    unnamed x7, local copies, waits for them, and re-layouts  9.45 us
    dot_general x1, matrix products, per_device(): lax.dot_general(piece, down_weight, last_dims, preferred_element_type=jnp...  8.82 us
  transfers between devices with their start and end apart: 6, of which 6 were waited for; matrix products, arithmetic and copies ran while one was open for 11% of the time, Pallas kernels for 0%

commit v1 on v0

--- a/solution.py
+++ b/solution.py
@@ -3,6 +3,24 @@
 import jax.numpy as jnp
 from jax import lax
 from jax.sharding import PartitionSpec as P
+
+
+def collect(array, axis, dim):
+    ways, here, turn = (lax.axis_size(axis), lax.axis_index(axis), array.shape[dim])
+    dims = [n * ways if d == dim else n for d, n in enumerate(array.shape)]
+    full = lax.dynamic_update_slice_in_dim(
+        jnp.zeros(dims, array.dtype), array, here * turn, axis=dim
+    )
+    going_up = going_down = array
+    for far in range(1, ways // 2 + 1):
+        going_up = lax.ppermute(going_up, axis, [(d, (d + 1) % ways) for d in range(ways)])
+        full = lax.dynamic_update_slice_in_dim(full, going_up, (here - far) % ways * turn, axis=dim)
+        if 2 * far < ways:
+            going_down = lax.ppermute(going_down, axis, [(d, (d - 1) % ways) for d in range(ways)])
+            full = lax.dynamic_update_slice_in_dim(
+                full, going_down, (here + far) % ways * turn, axis=dim
+            )
+    return full
 
 
 def gelu_pair(values):
@@ -19,7 +37,7 @@
 def per_device(inputs, cotangent, preactivation, up_weight, down_weight):
     inputs_all, cotangent_all = (
         lax.all_gather(inputs, "col", axis=0, tiled=True),
-        lax.all_gather(cotangent, "col", axis=0, tiled=True),
+        collect(cotangent, "col", 0),
     )
     total_tokens = inputs_all.shape[0]
     token_scale = 1.0 / math.sqrt(total_tokens)

time: 287 us -> 274 us (0.955)
  waiting for transfers between devices: 226 us -> 208 us
  starting transfers between devices: 0.24 us -> 5.58 us
    all_gather x1 -> x0, waiting for transfers between devices: 41.4 us -> none  [per_device(): lax.all_gather(cotangent, 'col', axis=0, tiled=True)]
    ppermute x0 -> x3, waiting for transfers between devices: none -> 25.8 us  [the longest x2 18.9 us: collect(): lax.ppermute(going_up, axis, [(d, (d + 1) % ways) for d in range(ways)])]
    ppermute x0 -> x3, starting transfers between devices: none -> 5.2 us  [the longest x2 3.11 us: collect(): lax.ppermute(going_up, axis, [(d, (d + 1) % ways) for d in range(ways)])]
    dot_general x1, matrix products: 8.82 us -> 5.43 us  [per_device(): lax.dot_general(piece, down_weight, last_dims, preferred_element_type=jnp...]
  transfers between devices with their start and end apart: 6 -> 8, of which waited for: 6 -> 8; matrix products, arithmetic and copies ran while one was open for 11% -> 13% of each run, Pallas kernels for 0% -> 0%
where the time goes in v1:
time: 274 us; the launch traced here: 273 us
  waiting for transfers between devices  208 us (76%)
  matrix products  30.8 us (11%)
  between operations  13.8 us (5%)
  local copies, waits for them, and re-layouts  9.46 us (3%)
  other arithmetic  5.61 us (2%)
  starting transfers between devices  5.58 us (2%)
    reduce_scatter x1, waiting for transfers between devices, per_device(): lax.psum_scatter(lax.dot_general(piece, down_weight, last_dims, preferred...  58.3 us
    reduce_scatter x1, waiting for transfers between devices, per_device(): lax.psum_scatter(lax.dot_general(piece, up_weight, last_dims, preferred_e...  55 us
    all_gather x1, waiting for transfers between devices, per_device(): lax.all_gather(inputs, 'col', axis=0, tiled=True)  30.3 us
    all_gather x1, waiting for transfers between devices, per_device(): lax.all_gather(pre_grad, 'row', axis=0, tiled=True)  27.1 us
    ppermute x2, waiting for transfers between devices, collect(): lax.ppermute(going_up, axis, [(d, (d + 1) % ways) for d in range(ways)])  18.9 us
    all_gather x1, waiting for transfers between devices, per_device(): lax.all_gather(activation, 'row', axis=0, tiled=True)  10.2 us
    dot_general x1, matrix products, per_device(): lax.dot_general(inputs_all, pre_grad_all, first_dims, preferred_element_t...  9.53 us
    unnamed x7, local copies, waits for them, and re-layouts  9.14 us
  transfers between devices with their start and end apart: 8, of which 8 were waited for; matrix products, arithmetic and copies ran while one was open for 13% of the time, Pallas kernels for 0%

profile of v1, /device:TPU:0, one launch (start us, length us, event | category | flops | bytes accessed | tf_op | source)
XLA Modules:
  0.0 273.3 jit_solution(12929812969807383026)
XLA Ops:
  7.2 0.0 copy-start.1
  7.2 0.0 reduce-scatter.3.cloned.1.call-start
  7.2 3.1 %collective-permute-start = (bf16[192,1024]{1,0:T(8,128)(2,1)}, bf16[192,1024]{1,0:T(8,128)(2,1)S(1)}, u32[]{:S(2)}, u32[]{:S(2)}) collective-permute-start(bf16[192,1024]{1,0:T(8,128)(2,1)} %param.6), channel_id=1, source_target_pairs={{0,1},{1,2},{2,3},{3,0},{4,5},{5,6},{6,7},{7,4},{8,9},{9,10},{10,1... | collective-permute-start | bytes 1179656 | tf_op jit(solution)/shard_map/ppermute | solution.py:16
  10.3 2.1 collective-permute-start.1
  12.4 10.2 %collective-permute-done = bf16[192,1024]{1,0:T(8,128)(2,1)S(1)} collective-permute-done((bf16[192,1024]{1,0:T(8,128)(2,1)}, bf16[192,1024]{1,0:T(8,128)(2,1)S(1)}, u32[]{:S(2)}, u32[]{:S(2)}) %collective-permute-start) | collective-permute-done | bytes 393248 | tf_op jit(solution)/shard_map/ppermute | solution.py:16
  22.6 0.0 collective-permute-start.2
  22.6 0.0 copy-start.2
  22.6 0.2 broadcast_in_dim.3
  22.8 0.0 copy-done.1
  22.9 6.9 %collective-permute-done.1 = bf16[192,1024]{1,0:T(8,128)(2,1)S(1)} collective-permute-done((bf16[192,1024]{1,0:T(8,128)(2,1)}, bf16[192,1024]{1,0:T(8,128)(2,1)S(1)}, u32[]{:S(2)}, u32[]{:S(2)}) %collective-permute-start.1) | collective-permute-done | bytes 393248 | tf_op jit(solution)/shard_map/ppermute | solution.py:19
  29.8 8.8 %collective-permute-done.2 = bf16[192,1024]{1,0:T(8,128)(2,1)S(1)} collective-permute-done((bf16[192,1024]{1,0:T(8,128)(2,1)S(1)}, bf16[192,1024]{1,0:T(8,128)(2,1)S(1)}, u32[]{:S(2)}, u32[]{:S(2)}) %collective-permute-start.2) | collective-permute-done | bytes 393248 | tf_op jit(solution)/shard_map/ppermute | solution.py:16
  38.6 0.0 copy-done.2
  38.6 5.4 %fusion.11 = f32[768,2048]{1,0:T(8,128)} fusion(bf16[768,1024]{1,0:T(8,128)(2,1)S(1)} %constant_dynamic-update-slice_fusion, bf16[2048,1024]{1,0:T(8,128)(2,1)S(1)} %copy-done.2), kind=kOutput, calls=%fused_computation.24 | convolution fusion | flops 3221225472 | bytes 12058624 | tf_op jit(solution)/shard_map/dot_general | solution.py:48
  44.1 0.0 copy-start
  44.1 0.0 reduce-scatter.3.cloned.1.call-update
  44.1 0.0 all-gather.4.cloned.1.call-start
  44.1 58.3 %reduce-scatter.3.cloned.1.call-done = f32[192,2048]{1,0:T(8,128)} async-done(((f32[768,2048]{1,0:T(8,128)}), f32[192,2048]{1,0:T(8,128)}) %reduce-scatter.3.cloned.1.call-update) | async-done | bytes 1572880 | tf_op jit(solution)/shard_map/reduce_scatter | solution.py:47
  102.4 0.0 copy-done
  102.4 3.7 %fusion.7 = (bf16[192,2048]{1,0:T(8,128)(2,1)}, bf16[192,2048]{1,0:T(8,128)(2,1)}) fusion(bf16[192,2048]{1,0:T(8,128)(2,1)S(1)} %copy-done, f32[192,2048]{1,0:T(8,128)} %reduce-scatter.3.cloned.1.call-done), kind=kLoop, calls=%fused_computation.16 | loop fusion | flops 8650752 | bytes 3932160 | tf_op jit(solution)/shard_map/convert_element_type | solution.py:54
  106.1 0.0 all-gather.4.cloned.1.call-update
  106.1 0.0 all-gather.6.cloned.1.call-start
  106.2 0.7 all-gather.6.cloned.1.call-update
  106.9 0.0 all-gather.8.cloned.1.call-start
  106.9 0.5 all-gather.8.cloned.1.call-update
  107.4 0.2 reduce-scatter.5.cloned.1.call-start
  107.7 27.1 %all-gather.4.cloned.1.call-done = bf16[768,2048]{1,0:T(8,128)(2,1)} async-done(((bf16[192,2048]{1,0:T(8,128)(2,1)}), bf16[768,2048]{1,0:T(8,128)(2,1)}) %all-gather.4.cloned.1.call-update) | async-done | bytes 3145744 | tf_op jit(solution)/shard_map/all_gather | solution.py:58
  134.8 8.3 %fusion.12 = f32[768,1024]{1,0:T(8,128)} fusion(bf16[768,2048]{1,0:T(8,128)(2,1)} %all-gather.4.cloned.1.call-done, bf16[1024,2048]{1,0:T(8,128)(2,1)} %param.8), kind=kOutput, calls=%fused_computation.25 | convolution fusion | flops 3221225472 | bytes 10485760 | tf_op jit(solution)/shard_map/dot_general | solution.py:62
  143.1 0.0 reduce-scatter.5.cloned.1.call-update
  143.1 30.3 %all-gather.6.cloned.1.call-done = bf16[768,1024]{1,0:T(8,128)(2,1)} async-done(((bf16[192,1024]{1,0:T(8,128)(2,1)}), bf16[768,1024]{1,0:T(8,128)(2,1)}) %all-gather.6.cloned.1.call-update) | async-done | bytes 1572880 | tf_op jit(solution)/shard_map/all_gather | solution.py:39
  173.4 9.5 %multiply_bitcast_fusion = f32[1024,2048]{0,1:T(8,128)} fusion(bf16[768,2048]{1,0:T(8,128)(2,1)} %all-gather.4.cloned.1.call-done, bf16[768,1024]{1,0:T(8,128)(2,1)} %all-gather.6.cloned.1.call-done), kind=kOutput, calls=%fused_computation | convolution fusion | flops 3223322624 | bytes 13107200 | tf_op jit(solution)/shard_map/dot_general | solution.py:68
  183.0 9.1 %copy.8 = f32[1024,2048]{1,0:T(8,128)} copy(f32[1024,2048]{0,1:T(8,128)} %multiply_bitcast_fusion) | data formatting | bytes 16777216
  192.1 10.2 %all-gather.8.cloned.1.call-done = bf16[768,2048]{1,0:T(8,128)(2,1)} async-done(((bf16[192,2048]{1,0:T(8,128)(2,1)}), bf16[768,2048]{1,0:T(8,128)(2,1)}) %all-gather.8.cloned.1.call-update) | async-done | bytes 3145744 | tf_op jit(solution)/shard_map/all_gather | solution.py:57
  202.3 7.6 %convolution_multiply_fusion = f32[2048,1024]{1,0:T(8,128)} fusion(bf16[768,2048]{1,0:T(8,128)(2,1)} %all-gather.8.cloned.1.call-done, bf16[768,1024]{1,0:T(8,128)(2,1)S(1)} %constant_dynamic-update-slice_fusion), kind=kOutput, calls=%fused_computation.1 | convolution fusion | flops 3223322624 | bytes 13107200 | tf_op jit(solution)/shard_map/dot_general | solution.py:72
  209.9 55.0 %reduce-scatter.5.cloned.1.call-done = f32[192,1024]{1,0:T(8,128)} async-done(((f32[768,1024]{1,0:T(8,128)}), f32[192,1024]{1,0:T(8,128)}) %reduce-scatter.5.cloned.1.call-update) | async-done | bytes 786448 | tf_op jit(solution)/shard_map/reduce_scatter | solution.py:61
  264.8 1.9 convert_element_type.14
  (4 shorter events, 0.1 us)
Async XLA Ops:
  7.2 15.6 %copy-start.1 = (bf16[192,1024]{1,0:T(8,128)(2,1)S(1)}, bf16[192,1024]{1,0:T(8,128)(2,1)}, u32[]{:S(2)}) copy-start(bf16[192,1024]{1,0:T(8,128)(2,1)} %param.6) | copy-start | bytes 1179652
  7.2 95.3 %reduce-scatter.3.cloned.1.call-start = ((), (), s32[]{:S(2)}) async-start(), calls=%async_computation.2 | async-start | bytes 7864320 | tf_op jit(solution)/shard_map/reduce_scatter | solution.py:47
  7.2 15.3 %collective-permute-start = (bf16[192,1024]{1,0:T(8,128)(2,1)}, bf16[192,1024]{1,0:T(8,128)(2,1)S(1)}, u32[]{:S(2)}, u32[]{:S(2)}) collective-permute-start(bf16[192,1024]{1,0:T(8,128)(2,1)} %param.6), channel_id=1, source_target_pairs={{0,1},{1,2},{2,3},{3,0},{4,5},{5,6},{6,7},{7,4},{8,9},{9,10},{10,1... | collective-permute-start | bytes 1179656 | tf_op jit(solution)/shard_map/ppermute | solution.py:16
  10.3 19.5 %collective-permute-start.1 = (bf16[192,1024]{1,0:T(8,128)(2,1)}, bf16[192,1024]{1,0:T(8,128)(2,1)S(1)}, u32[]{:S(2)}, u32[]{:S(2)}) collective-permute-start(bf16[192,1024]{1,0:T(8,128)(2,1)} %param.6), channel_id=1, source_target_pairs={{0,3},{1,0},{2,1},{3,2},{4,7},{5,4},{6,5},{7,6},{8,11},{9,8},{10,9... | collective-permute-start | bytes 1179656 | tf_op jit(solution)/shard_map/ppermute | solution.py:19
  22.6 16.0 %collective-permute-start.2 = (bf16[192,1024]{1,0:T(8,128)(2,1)S(1)}, bf16[192,1024]{1,0:T(8,128)(2,1)S(1)}, u32[]{:S(2)}, u32[]{:S(2)}) collective-permute-start(bf16[192,1024]{1,0:T(8,128)(2,1)S(1)} %collective-permute-done), channel_id=1, source_target_pairs={{0,1},{1,2},{2,3},{3,0},{4,5},{5,6},{6,7},{7,4},{8,9},{9,10},{10,1... | collective-permute-start | bytes 1179656 | tf_op jit(solution)/shard_map/ppermute | solution.py:16
  22.6 16.0 %copy-start.2 = (bf16[2048,1024]{1,0:T(8,128)(2,1)S(1)}, bf16[2048,1024]{1,0:T(8,128)(2,1)}, u32[]{:S(2)}) copy-start(bf16[2048,1024]{1,0:T(8,128)(2,1)} %param.9) | copy-start | bytes 12582916
  44.1 58.4 %copy-start = (bf16[192,2048]{1,0:T(8,128)(2,1)S(1)}, bf16[192,2048]{1,0:T(8,128)(2,1)}, u32[]{:S(2)}) copy-start(bf16[192,2048]{1,0:T(8,128)(2,1)} %param.7) | copy-start | bytes 2359300
  44.1 90.7 %all-gather.4.cloned.1.call-start = ((), (), s32[]{:S(2)}) async-start(), calls=%async_computation.3 | async-start | bytes 3932160 | tf_op jit(solution)/shard_map/all_gather | solution.py:58
  106.1 67.3 %all-gather.6.cloned.1.call-start = ((), (), s32[]{:S(2)}) async-start(), calls=%async_computation.5 | async-start | bytes 1966080 | tf_op jit(solution)/shard_map/all_gather | solution.py:39
  106.9 95.4 %all-gather.8.cloned.1.call-start = ((), (), s32[]{:S(2)}) async-start(), calls=%async_computation.6 | async-start | bytes 3932160 | tf_op jit(solution)/shard_map/all_gather | solution.py:57
  107.4 157.4 %reduce-scatter.5.cloned.1.call-start = ((), (), s32[]{:S(2)}) async-start(), calls=%async_computation.4 | async-start | bytes 3932160 | tf_op jit(solution)/shard_map/reduce_scatter | solution.py:61
Sparse Core Ops, SparseCore 0:
  44.2 58.1 reduce-scatter.2
  106.3 28.5 all-gather.3
  136.4 37.0 all-gather.5
  174.9 27.3 all-gather.7
  204.4 60.3 reduce-scatter.4
